TPU v7x, 512 devices: a whole 4x8x8 slice. The times are simulated.
512 devices in a mesh: lon: 64 (over z_hi, x, y), ch: 8 (over z_lo, core).
Axes of the slice: x: 4, y: 8, z: 8 (z_hi: 2, z_lo: 4; z = z_hi * 4 + z_lo), core: 2. Of those that a mesh axis runs over, the one named last changes fastest.
Arguments:
- coarse: bfloat16 [16, 4, 256, 1024], P(None, None, 'lon', 'ch'), may hold values from -6 to 6
- up_kernel: bfloat16 [4, 4, 1024, 512], P(None, None, 'ch', 'lon'), may hold values from -0.09375 to 0.09375
- up_bias: float32 [512], replicated, may hold values from -3 to 3
- conv_kernel: bfloat16 [3, 3, 512, 512], P(None, None, 'lon'), may hold values from -0.09375 to 0.09375
- conv_bias: float32 [512], replicated, may hold values from -3 to 3
Outputs:
- fine_out: bfloat16 [32, 4, 512, 512], P('ch', None, 'lon')
All inputs are finite; a program needn't handle non-finite values.
Results may differ from a plain program's by a relative error of at most 0.015.
Values may be sent and summed in bfloat16 or wider, within the bound.
A program may use at most 64 MiB of HBM per device.

v0:
```python
import jax
import jax.numpy as jnp
from jax import lax
from jax.sharding import PartitionSpec as P

TAPS = (((1, 1), (3, 0)), ((2, 1), (0, 2)))


def padded_2(block, sides, width, periodic):
    for axis, dim in sides:
        count = lax.axis_size(axis)
        forward = [(i, i + 1) for i in range(count - 1)]
        if periodic:
            forward.append((count - 1, 0))
        backward = [(target, source) for source, target in forward]
        low = lax.ppermute(
            lax.slice_in_dim(block, block.shape[dim] - width, None, axis=dim), axis, forward
        )
        high = lax.ppermute(lax.slice_in_dim(block, 0, width, axis=dim), axis, backward)
        block = jnp.concatenate([low, block, high], axis=dim)
    return block


def tap_dot(piece, weight):
    return jnp.einsum("rbjc,cn->rbjn", piece, weight, preferred_element_type=jnp.float32)


def upsample(padded, lon_count, weights):
    rows = padded.shape[0] - 2
    batch = padded.shape[1]
    phases = []
    for p in range(2):
        columns = []
        for q in range(2):
            total = None
            for a, row_off in TAPS[p]:
                for c, col_off in TAPS[q]:
                    piece = padded[row_off : row_off + rows, :, col_off : col_off + lon_count, :]
                    term = tap_dot(piece, weights[a, c])
                    total = term if total is None else total + term
            columns.append(total)
        phases.append(jnp.stack(columns, axis=3))
    stacked = jnp.stack(phases, axis=1)
    return stacked.reshape(2 * rows, batch, 2 * lon_count, weights.shape[-1])


def shards(coarse, up_kernel, up_bias, conv_kernel, conv_bias):
    lon_dev = coarse.shape[2]
    row_padded = jnp.pad(coarse, ((1, 1), (0, 0), (0, 0), (0, 0)))
    source = jnp.pad(row_padded, ((0, 0), (0, 0), (2, 2), (0, 0)))
    count = lon_dev + 2
    up_full = lax.all_gather(up_kernel, "lon", axis=3, tiled=True)
    partial_value = upsample(source, count, up_full)
    local_fine = partial_value[:, :, 2 : 2 * lon_dev + 2]
    spill = jnp.concatenate(
        [partial_value[:, :, 1:2], partial_value[:, :, 2 * lon_dev + 2 : 2 * lon_dev + 3]], axis=2
    )
    beside_all = padded_2(spill.astype(jnp.bfloat16), (("lon", 2),), 1, True).astype(spill.dtype)
    local_fine = local_fine.at[:, :, 0].add(beside_all[:, :, 0])
    local_fine = local_fine.at[:, :, -1].add(beside_all[:, :, 3])
    summed = lax.psum_scatter(
        local_fine.astype(jnp.bfloat16), "ch", scatter_dimension=0, tiled=True
    ).astype(jnp.float32)
    hidden = jax.nn.gelu(summed + up_bias, approximate=False).astype(jnp.bfloat16)
    widened = padded_2(hidden, (("lon", 2),), 1, True)
    framed = padded_2(widened, (("ch", 0),), 1, False)
    weights = lax.all_gather(conv_kernel, "lon", axis=2, tiled=True)
    band_rows = hidden.shape[0]
    fine_cols = hidden.shape[2]
    result = jnp.zeros(hidden.shape, jnp.float32) + conv_bias
    for d in range(3):
        for t in range(3):
            result = result + tap_dot(
                framed[d : d + band_rows, :, t : t + fine_cols, :], weights[d, t]
            )
    return result.astype(jnp.bfloat16)


def solution(mesh):
    return jax.shard_map(
        shards,
        mesh=mesh,
        in_specs=(
            P(None, None, "lon", "ch"),
            P(None, None, "ch", "lon"),
            P(),
            P(None, None, "lon", None),
            P(),
        ),
        out_specs=P("ch", None, "lon", None),
        check_vma=False,
    )
```

profile of v0, /device:TPU:2, one launch (start us, length us, event | category | flops | bytes accessed | tf_op | source)
XLA Modules:
  0.0 451.6 jit_solution(3137635655831633041)
XLA Ops:
  6.5 1.4 copy.15
  8.0 0.9 copy.14
  8.9 146.6 %all-gather.3.cloned.1.call-done = bf16[4,4,128,512]{2,1,0,3:T(4,128)(2,1)} async-done(((bf16[4,4,128,8]{2,1,0,3:T(4,128)(2,1)}), bf16[4,4,128,512]{2,1,0,3:T(4,128)(2,1)}) %all-gather.3.cloned.1.call-update) | async-done | bytes 2097168 | tf_op jit(solution)/shard_map/all_gather | solution.py:52
  155.5 8.8 %fusion.77 = (bf16[1,1,128,512]{2,1,0,3:T(2,128)(2,1)S(1)}, bf16[1,1,128,512]{2,1,0,3:T(2,128)(2,1)S(1)}, bf16[1,1,128,512]{2,1,0,3:T(2,128)(2,1)}, bf16[1,1,128...) fusion(bf16[4,4,128,512]{2,1,0,3:T(4,128)(2,1)} %all-gather.3.c, ...), kind=kLoop, calls=%fused_computation.133 | loop fusion | bytes 4194304 | tf_op jit(solution)/shard_map/slice | solution.py:39
  164.3 0.8 copy.69
  165.1 0.8 copy.70
  165.9 0.8 copy.71
  166.6 0.8 copy.72
  167.4 0.8 copy.73
  168.2 1.1 fusion.50
  169.4 1.1 fusion.45
  170.5 1.7 copy.74
  172.2 0.8 copy.75
  173.0 0.8 copy.76
  173.8 0.8 copy.61
  174.6 1.1 fusion.60
  175.7 1.7 copy.62
  177.5 0.8 copy.63
  178.3 0.8 copy.64
  179.0 0.8 copy.65
  179.8 1.1 fusion.55
  181.0 1.7 copy.66
  182.7 1.7 copy.67
  184.4 0.8 copy.68
  185.2 1.2 convolution_add_fusion.5
  186.4 1.2 convolution_add_fusion.4
  187.7 0.3 fusion.1
  190.1 0.2 fusion.2
  190.3 0.4 maximum_bitcast_fusion
  190.7 0.3 pad_maximum_fusion
  191.0 2.0 copy.32
  193.0 0.9 copy.78
  193.9 0.5 fusion.76
  194.5 2.4 collective-permute-start
  196.8 5.8 %collective-permute-start.1 = (bf16[32,4,1,512]{3,2,1,0:T(2,128)(2,1)S(1)}, bf16[32,4,1,512]{3,2,1,0:T(2,128)(2,1)S(1)}, u32[]{:S(2)}, u32[]{:S(2)}) collective-permute-start(bf16[32,4,1,512]{3,2,1,0:T(2,128)(2,1)S(1)} %get-tuple-element.30), channel_id=1, source_target_pairs={{8,0},{16,8},{24,16},{32,24},{40,32},{48,40},{56,48},{64,56},{72,6... | collective-permute-start | bytes 393224 | tf_op jit(solution)/shard_map/ppermute | solution.py:19
  202.6 1.3 copy.33
  203.9 0.5 slice.296
  204.4 0.4 collective-permute-done
  204.8 1.5 collective-permute-done.1
  206.3 1.4 convert_add_fusion
  207.7 2.1 scatter-add.6
  209.8 1.4 fusion.23
  211.2 2.1 scatter-add.9
  213.3 1.2 convert_element_type.21
  214.5 0.7 all-gather.5.cloned.1.call-update
  215.2 47.2 %reduce-scatter.2.cloned.1.call-done = bf16[4,4,8,512]{3,2,1,0:T(8,128)(2,1)} async-done(((bf16[32,4,8,512]{3,2,1,0:T(8,128)(2,1)}), bf16[4,4,8,512]{3,2,1,0:T(8,128)(2,1)}) %reduce-scatter.2.cloned.1.call-update) | async-done | bytes 131088 | tf_op jit(solution)/shard_map/reduce_scatter | solution.py:61
  262.4 1.5 fusion.21
  263.9 3.4 collective-permute-start.2
  267.3 4.6 %collective-permute-start.3 = (bf16[4,4,1,512]{3,2,1,0:T(2,128)(2,1)S(1)}, bf16[4,4,1,512]{3,2,1,0:T(2,128)(2,1)S(1)}, u32[]{:S(2)}, u32[]{:S(2)}) collective-permute-start(bf16[4,4,1,512]{3,2,1,0:T(2,128)(2,1)S(1)} %get-tuple-element.52), channel_id=1, source_target_pairs={{8,0},{16,8},{24,16},{32,24},{40,32},{48,40},{56,48},{64,56},{72,6... | collective-permute-start | bytes 49160 | tf_op jit(solution)/shard_map/ppermute | solution.py:19
  271.9 1.6 collective-permute-done.3
  273.6 1.3 collective-permute-start.4
  274.9 1.3 collective-permute-start.5
  276.2 1.8 collective-permute-done.5
  278.0 0.2 maximum_maximum_fusion
  278.3 154.6 %all-gather.5.cloned.1.call-done = bf16[3,3,512,512]{3,2,1,0:T(8,128)(2,1)} async-done(((bf16[3,3,8,512]{3,2,1,0:T(8,128)(2,1)}), bf16[3,3,512,512]{3,2,1,0:T(8,128)(2,1)}) %all-gather.5.cloned.1.call-update) | async-done | bytes 4718608 | tf_op jit(solution)/shard_map/all_gather | solution.py:67
  432.8 1.3 fusion.16
  434.1 1.3 fusion.17
  435.4 1.3 fusion.18
  436.7 1.3 fusion.15
  438.0 1.3 fusion.13
  439.2 1.3 fusion.14
  440.5 1.3 fusion.12
  441.8 1.3 fusion.10
  443.1 2.0 fusion.11
  (41 shorter events, 2.2 us)
Async XLA Ops:
  6.5 149.0 %all-gather.3.cloned.1.call-start = ((), (), s32[]{:S(2)}) async-start(), calls=%async_computation.1 | async-start | bytes 2129920 | tf_op jit(solution)/shard_map/all_gather | solution.py:52
  7.9 254.4 %reduce-scatter.2.cloned.1.call-start = ((), (), s32[]{:S(2)}) async-start(), calls=%async_computation.2 | async-start | bytes 1179648 | tf_op jit(solution)/shard_map/reduce_scatter | solution.py:61
  185.2 2.4 copy-start
  185.2 2.7 copy-start.2
  185.2 3.0 copy-start.3
  186.4 2.0 copy-start.1
  187.6 1.1 copy-start.5
  187.9 1.1 copy-start.6
  188.2 1.1 copy-start.4
  188.5 1.1 copy-start.8
  188.7 1.1 copy-start.9
  189.0 1.0 copy-start.7
  194.5 10.4 %collective-permute-start = (bf16[32,4,1,512]{3,2,1,0:T(2,128)(2,1)S(1)}, bf16[32,4,1,512]{3,2,1,0:T(2,128)(2,1)S(1)}, u32[]{:S(2)}, u32[]{:S(2)}) collective-permute-start(bf16[32,4,1,512]{3,2,1,0:T(2,128)(2,1)S(1)} %get-tuple-element.29), channel_id=1, source_target_pairs={{0,8},{8,16},{16,24},{24,32},{32,40},{40,48},{48,56},{56,64},{64,7... | collective-permute-start | bytes 393224 | tf_op jit(solution)/shard_map/ppermute | solution.py:16
  196.8 9.5 %collective-permute-start.1 = (bf16[32,4,1,512]{3,2,1,0:T(2,128)(2,1)S(1)}, bf16[32,4,1,512]{3,2,1,0:T(2,128)(2,1)S(1)}, u32[]{:S(2)}, u32[]{:S(2)}) collective-permute-start(bf16[32,4,1,512]{3,2,1,0:T(2,128)(2,1)S(1)} %get-tuple-element.30), channel_id=1, source_target_pairs={{8,0},{16,8},{24,16},{32,24},{40,32},{48,40},{56,48},{64,56},{72,6... | collective-permute-start | bytes 393224 | tf_op jit(solution)/shard_map/ppermute | solution.py:19
  209.8 52.6 %copy-start.10 = (f32[512]{0:T(512)S(1)}, f32[512]{0:T(512)}, u32[]{:S(2)}) copy-start(f32[512]{0:T(512)} %param.11) | copy-start | bytes 6148
  214.5 218.3 %all-gather.5.cloned.1.call-start = ((), (), s32[]{:S(2)}) async-start(), calls=%async_computation.3 | async-start | bytes 4792320 | tf_op jit(solution)/shard_map/all_gather | solution.py:67
  263.9 8.0 %collective-permute-start.2 = (bf16[4,4,1,512]{3,2,1,0:T(2,128)(2,1)S(1)}, bf16[4,4,1,512]{3,2,1,0:T(2,128)(2,1)S(1)}, u32[]{:S(2)}, u32[]{:S(2)}) collective-permute-start(bf16[4,4,1,512]{3,2,1,0:T(2,128)(2,1)S(1)} %get-tuple-element.51), channel_id=1, source_target_pairs={{0,8},{8,16},{16,24},{24,32},{32,40},{40,48},{48,56},{56,64},{64,7... | collective-permute-start | bytes 49160 | tf_op jit(solution)/shard_map/ppermute | solution.py:16
  267.3 6.1 %collective-permute-start.3 = (bf16[4,4,1,512]{3,2,1,0:T(2,128)(2,1)S(1)}, bf16[4,4,1,512]{3,2,1,0:T(2,128)(2,1)S(1)}, u32[]{:S(2)}, u32[]{:S(2)}) collective-permute-start(bf16[4,4,1,512]{3,2,1,0:T(2,128)(2,1)S(1)} %get-tuple-element.52), channel_id=1, source_target_pairs={{8,0},{16,8},{24,16},{32,24},{40,32},{48,40},{56,48},{64,56},{72,6... | collective-permute-start | bytes 49160 | tf_op jit(solution)/shard_map/ppermute | solution.py:19
  273.6 2.6 collective-permute-start.4
  274.9 3.1 collective-permute-start.5
  278.3 163.5 %copy-start.11 = (f32[512]{0:T(512)S(1)}, f32[512]{0:T(512)}, u32[]{:S(2)}) copy-start(f32[512]{0:T(512)} %param.13) | copy-start | bytes 6148
Sparse Core Ops, SparseCore 0:
  11.8 143.6 all-gather.2
  214.6 47.7 reduce-scatter.1
  266.7 166.0 all-gather.4
where the time goes:
time: 453 us; the launch traced here: 452 us
  waiting for transfers between devices  354 us (78%)
  local copies, waits for them, and re-layouts  36.9 us (8%)
  matrix products  21.6 us (5%)
  starting transfers between devices  18.8 us (4%)
  between operations  13.6 us (3%)
  other arithmetic  6.35 us (1%)
    all_gather x1, waiting for transfers between devices, shards(): weights = lax.all_gather(conv_kernel, 'lon', axis=2, tiled=True)  155 us
    all_gather x1, waiting for transfers between devices, shards(): up_full = lax.all_gather(up_kernel, 'lon', axis=3, tiled=True)  147 us
    reduce_scatter x1, waiting for transfers between devices, shards(): lax.psum_scatter(local_fine.astype(jnp.bfloat16), 'ch', scatter_dimension...  47.2 us
    dot_general x25, matrix products, tap_dot(): jnp.einsum('rbjc,cn->rbjn', piece, weight, preferred_element_type=jnp.flo...  21.6 us
    unnamed x42, local copies, waits for them, and re-layouts  18.6 us
    ppermute x3, starting transfers between devices, padded_2(): lax.ppermute(lax.slice_in_dim(block, 0, width, axis=dim), axis, backward)  11.6 us
  transfers between devices with their start and end apart: 9, of which 7 were waited for; matrix products, arithmetic and copies ran while one was open for 1% of the time, Pallas kernels for 0%

commit v1 on v0

--- a/solution.py
+++ b/solution.py
@@ -64,7 +64,10 @@
     hidden = jax.nn.gelu(summed + up_bias, approximate=False).astype(jnp.bfloat16)
     widened = padded_2(hidden, (("lon", 2),), 1, True)
     framed = padded_2(widened, (("ch", 0),), 1, False)
-    weights = lax.all_gather(conv_kernel, "lon", axis=2, tiled=True)
+    count_2 = lax.axis_size("lon")
+    blocks = jnp.stack([conv_kernel for _ in range(count_2)])
+    blocks = lax.all_to_all(blocks, "lon", split_axis=0, concat_axis=0)
+    weights = jnp.concatenate(blocks, axis=2)
     band_rows = hidden.shape[0]
     fine_cols = hidden.shape[2]
     result = jnp.zeros(hidden.shape, jnp.float32) + conv_bias

time: 453 us -> 374 us (0.83)
  the two profiles are of different devices: /device:TPU:2 before, /device:TPU:63 now
where the time goes in v1:
time: 374 us; the launch traced here: 373 us
  waiting for transfers between devices  273 us (73%)
  starting transfers between devices  39.6 us (11%)
  local copies, waits for them, and re-layouts  33.4 us (9%)
  between operations  13.9 us (4%)
  matrix products  6.78 us (2%)
  other arithmetic  6.54 us (2%)
    all_gather x1, waiting for transfers between devices, shards(): up_full = lax.all_gather(up_kernel, 'lon', axis=3, tiled=True)  206 us
    reduce_scatter x1, waiting for transfers between devices, shards(): lax.psum_scatter(local_fine.astype(jnp.bfloat16), 'ch', scatter_dimension...  43.3 us
    ppermute x3, waiting for transfers between devices, padded_2(): lax.ppermute(lax.slice_in_dim(block, 0, width, axis=dim), axis, backward)  23.7 us
    all_to_all x1, starting transfers between devices, shards(): blocks = lax.all_to_all(blocks, 'lon', split_axis=0, concat_axis=0)  18.1 us
    ppermute x3, starting transfers between devices, padded_2(): lax.ppermute(lax.slice_in_dim(block, block.shape[dim] - width, None, axis...  11.9 us
    ppermute x3, starting transfers between devices, padded_2(): lax.ppermute(lax.slice_in_dim(block, 0, width, axis=dim), axis, backward)  9.54 us
    unnamed x32, local copies, waits for them, and re-layouts  8.98 us
    slice x1, local copies, waits for them, and re-layouts, upsample(): term = tap_dot(piece, weights[a, c])  8.85 us
  transfers between devices with their start and end apart: 9, of which 5 were waited for; matrix products, arithmetic and copies ran while one was open for 11% of the time, Pallas kernels for 0%

profile of v1, /device:TPU:63, one launch (start us, length us, event | category | flops | bytes accessed | tf_op | source)
XLA Modules:
  0.0 373.1 jit_solution(9731613115937419185)
XLA Ops:
  6.5 1.4 copy.15
  7.9 3.4 stack.29
  11.3 18.1 %all-to-all-start = ((bf16[64,3,3,8,512]{4,3,2,1,0:T(8,128)(2,1)}), bf16[64,3,3,8,512]{4,3,2,1,0:T(8,128)(2,1)}, u32[]{:S(2)}, u32[]{:S(2)}) async-start(bf16[64,3,3,8,512]{4,3,2,1,0:T(8,128)(2,1)} %stack.29), calls=%async_computation.1 | async-start | bytes 9437184 | tf_op jit(solution)/shard_map/all_to_all | solution.py:69
  29.5 205.8 %all-gather.2.cloned.1.call-done = bf16[4,4,128,512]{2,1,0,3:T(4,128)(2,1)} async-done(((bf16[4,4,128,8]{2,1,0,3:T(4,128)(2,1)}), bf16[4,4,128,512]{2,1,0,3:T(4,128)(2,1)}) %all-gather.2.cloned.1.call-update) | async-done | bytes 2097168 | tf_op jit(solution)/shard_map/all_gather | solution.py:52
  235.3 8.9 %fusion.77 = (bf16[1,1,128,512]{2,1,0,3:T(2,128)(2,1)}, bf16[1,1,128,512]{2,1,0,3:T(2,128)(2,1)}, bf16[1,1,128,512]{2,1,0,3:T(2,128)(2,1)}, bf16[1,1,128,512]{2,...) fusion(bf16[4,4,128,512]{2,1,0,3:T(4,128)(2,1)} %all-gather.2.c, ...), kind=kLoop, calls=%fused_computation.134 | loop fusion | bytes 4194304 | tf_op jit(solution)/shard_map/slice | solution.py:39
  244.2 1.7 copy.65
  245.9 1.7 copy.76
  247.7 1.7 copy.75
  249.4 0.8 copy.74
  250.3 0.1 copy.72
  250.5 0.1 copy.71
  250.6 0.1 copy.70
  250.7 0.1 copy.69
  250.9 0.1 copy.68
  251.8 0.2 fusion.60
  252.1 0.2 convolution_add_fusion.11
  252.3 0.2 convolution_add_fusion.10
  252.6 0.2 fusion.3
  252.8 0.2 fusion.55
  253.1 0.2 convolution_add_fusion.8
  253.3 0.2 convolution_add_fusion.7
  253.6 0.2 fusion.2
  253.9 0.2 fusion.50
  254.1 0.2 convolution_add_fusion.5
  254.4 0.2 convolution_add_fusion.4
  254.6 0.2 fusion.1
  254.9 0.2 fusion.45
  255.1 0.2 convolution_add_fusion.2
  255.4 0.2 convolution_add_fusion.1
  255.6 0.2 fusion
  255.9 0.6 maximum_bitcast_fusion
  256.5 0.3 pad_maximum_fusion
  256.8 2.0 copy.32
  258.8 0.9 copy.80
  259.7 0.5 fusion.76
  260.2 1.9 collective-permute-start
  262.2 3.5 collective-permute-start.1
  265.7 1.3 copy.33
  267.0 0.5 slice.296
  267.5 11.3 %collective-permute-done.1 = bf16[32,4,1,512]{3,2,1,0:T(2,128)(2,1)S(1)} collective-permute-done((bf16[32,4,1,512]{3,2,1,0:T(2,128)(2,1)S(1)}, bf16[32,4,1,512]{3,2,1,0:T(2,128)(2,1)S(1)}, u32[]{:S(2)}, u32[]{:S(2)}) %collective-permute-start.1) | collective-permute-done | bytes 131104 | tf_op jit(solution)/shard_map/ppermute | solution.py:19
  278.8 1.4 convert_add_fusion
  280.2 2.1 scatter-add.6
  282.3 1.4 fusion.23
  283.7 2.1 scatter-add.9
  285.8 1.2 convert_element_type.21
  287.0 43.3 %reduce-scatter.2.cloned.1.call-done = bf16[4,4,8,512]{3,2,1,0:T(8,128)(2,1)} async-done(((bf16[32,4,8,512]{3,2,1,0:T(8,128)(2,1)}), bf16[4,4,8,512]{3,2,1,0:T(8,128)(2,1)}) %reduce-scatter.2.cloned.1.call-update) | async-done | bytes 131088 | tf_op jit(solution)/shard_map/reduce_scatter | solution.py:61
  330.3 1.5 fusion.21
  331.8 7.4 %collective-permute-start.2 = (bf16[4,4,1,512]{3,2,1,0:T(2,128)(2,1)S(1)}, bf16[4,4,1,512]{3,2,1,0:T(2,128)(2,1)S(1)}, u32[]{:S(2)}, u32[]{:S(2)}) collective-permute-start(bf16[4,4,1,512]{3,2,1,0:T(2,128)(2,1)S(1)} %get-tuple-element.51), channel_id=1, source_target_pairs={{0,8},{8,16},{16,24},{24,32},{32,40},{40,48},{48,56},{56,64},{64,7... | collective-permute-start | bytes 49160 | tf_op jit(solution)/shard_map/ppermute | solution.py:16
  339.3 1.9 collective-permute-start.3
  341.2 10.9 %collective-permute-done.3 = bf16[4,4,1,512]{3,2,1,0:T(2,128)(2,1)S(1)} collective-permute-done((bf16[4,4,1,512]{3,2,1,0:T(2,128)(2,1)S(1)}, bf16[4,4,1,512]{3,2,1,0:T(2,128)(2,1)S(1)}, u32[]{:S(2)}, u32[]{:S(2)}) %collective-permute-start.3) | collective-permute-done | bytes 16416 | tf_op jit(solution)/shard_map/ppermute | solution.py:19
  352.2 2.5 collective-permute-start.4
  354.8 4.1 %collective-permute-start.5 = (bf16[1,4,10,512]{3,2,1,0:T(8,128)(2,1)S(1)}, bf16[1,4,10,512]{3,2,1,0:T(8,128)(2,1)S(1)}, u32[]{:S(2)}, u32[]{:S(2)}) collective-permute-start(bf16[1,4,10,512]{3,2,1,0:T(8,128)(2,1)S(1)} %get-tuple-element.50), channel_id=1, source_target_pairs={{1,0},{2,1},{3,2},{4,3},{5,4},{6,5},{7,6},{9,8},{10,9},{11,10},{12... | collective-permute-start | bytes 122888 | tf_op jit(solution)/shard_map/ppermute | solution.py:19
  358.8 1.5 collective-permute-done.5
  360.3 0.2 maximum_maximum_fusion
  360.6 2.7 copy_bitcast_fusion
  363.4 0.2 fusion.12
  363.6 0.2 fusion.13
  363.8 0.2 fusion.14
  364.1 0.2 fusion.15
  364.3 0.2 fusion.17
  364.6 0.2 fusion.18
  364.8 0.2 fusion.16
  365.1 0.3 fusion.10
  365.4 0.9 fusion.11
  (32 shorter events, 1.2 us)
Async XLA Ops:
  6.5 228.8 %all-gather.2.cloned.1.call-start = ((), (), s32[]{:S(2)}) async-start(), calls=%async_computation.2 | async-start | bytes 2129920 | tf_op jit(solution)/shard_map/all_gather | solution.py:52
  11.3 18.1 %copy-start.4 = (bf16[16,4,4,128]{3,2,1,0:T(4,128)(2,1)S(1)}, bf16[16,4,4,128]{3,2,1,0:T(4,128)(2,1)}, u32[]{:S(2)}) copy-start(bf16[16,4,4,128]{3,2,1,0:T(4,128)(2,1)} %param.9) | copy-start | bytes 196612
  11.3 349.3 %all-to-all-start = ((bf16[64,3,3,8,512]{4,3,2,1,0:T(8,128)(2,1)}), bf16[64,3,3,8,512]{4,3,2,1,0:T(8,128)(2,1)}, u32[]{:S(2)}, u32[]{:S(2)}) async-start(bf16[64,3,3,8,512]{4,3,2,1,0:T(8,128)(2,1)} %stack.29), calls=%async_computation.1 | async-start | bytes 9437184 | tf_op jit(solution)/shard_map/all_to_all | solution.py:69
  29.4 300.9 %reduce-scatter.2.cloned.1.call-start = ((), (), s32[]{:S(2)}) async-start(), calls=%async_computation.3 | async-start | bytes 1179648 | tf_op jit(solution)/shard_map/reduce_scatter | solution.py:61
  250.2 2.4 copy-start.3
  253.3 1.5 copy-start.2
  253.6 1.5 copy-start.1
  253.9 1.5 copy-start
  260.2 7.3 %collective-permute-start = (bf16[32,4,1,512]{3,2,1,0:T(2,128)(2,1)S(1)}, bf16[32,4,1,512]{3,2,1,0:T(2,128)(2,1)S(1)}, u32[]{:S(2)}, u32[]{:S(2)}) collective-permute-start(bf16[32,4,1,512]{3,2,1,0:T(2,128)(2,1)S(1)} %get-tuple-element.29), channel_id=1, source_target_pairs={{0,8},{8,16},{16,24},{24,32},{32,40},{40,48},{48,56},{56,64},{64,7... | collective-permute-start | bytes 393224 | tf_op jit(solution)/shard_map/ppermute | solution.py:16
  262.2 16.6 %collective-permute-start.1 = (bf16[32,4,1,512]{3,2,1,0:T(2,128)(2,1)S(1)}, bf16[32,4,1,512]{3,2,1,0:T(2,128)(2,1)S(1)}, u32[]{:S(2)}, u32[]{:S(2)}) collective-permute-start(bf16[32,4,1,512]{3,2,1,0:T(2,128)(2,1)S(1)} %get-tuple-element.30), channel_id=1, source_target_pairs={{8,0},{16,8},{24,16},{32,24},{40,32},{48,40},{56,48},{64,56},{72,6... | collective-permute-start | bytes 393224 | tf_op jit(solution)/shard_map/ppermute | solution.py:19
  267.5 62.8 %copy-start.5 = (f32[512]{0:T(512)S(1)}, f32[512]{0:T(512)}, u32[]{:S(2)}) copy-start(f32[512]{0:T(512)} %param.11) | copy-start | bytes 6148
  331.8 9.4 %collective-permute-start.2 = (bf16[4,4,1,512]{3,2,1,0:T(2,128)(2,1)S(1)}, bf16[4,4,1,512]{3,2,1,0:T(2,128)(2,1)S(1)}, u32[]{:S(2)}, u32[]{:S(2)}) collective-permute-start(bf16[4,4,1,512]{3,2,1,0:T(2,128)(2,1)S(1)} %get-tuple-element.51), channel_id=1, source_target_pairs={{0,8},{8,16},{16,24},{24,32},{32,40},{40,48},{48,56},{56,64},{64,7... | collective-permute-start | bytes 49160 | tf_op jit(solution)/shard_map/ppermute | solution.py:16
  339.3 12.9 %collective-permute-start.3 = (bf16[4,4,1,512]{3,2,1,0:T(2,128)(2,1)S(1)}, bf16[4,4,1,512]{3,2,1,0:T(2,128)(2,1)S(1)}, u32[]{:S(2)}, u32[]{:S(2)}) collective-permute-start(bf16[4,4,1,512]{3,2,1,0:T(2,128)(2,1)S(1)} %get-tuple-element.52), channel_id=1, source_target_pairs={{8,0},{16,8},{24,16},{32,24},{40,32},{48,40},{56,48},{64,56},{72,6... | collective-permute-start | bytes 49160 | tf_op jit(solution)/shard_map/ppermute | solution.py:19
  352.2 6.6 %collective-permute-start.4 = (bf16[1,4,10,512]{3,2,1,0:T(8,128)(2,1)S(1)}, bf16[1,4,10,512]{3,2,1,0:T(8,128)(2,1)S(1)}, u32[]{:S(2)}, u32[]{:S(2)}) collective-permute-start(bf16[1,4,10,512]{3,2,1,0:T(8,128)(2,1)S(1)} %get-tuple-element.49), channel_id=1, source_target_pairs={{0,1},{1,2},{2,3},{3,4},{4,5},{5,6},{6,7},{8,9},{9,10},{10,11},{11... | collective-permute-start | bytes 122888 | tf_op jit(solution)/shard_map/ppermute | solution.py:16
  354.8 5.6 %collective-permute-start.5 = (bf16[1,4,10,512]{3,2,1,0:T(8,128)(2,1)S(1)}, bf16[1,4,10,512]{3,2,1,0:T(8,128)(2,1)S(1)}, u32[]{:S(2)}, u32[]{:S(2)}) collective-permute-start(bf16[1,4,10,512]{3,2,1,0:T(8,128)(2,1)S(1)} %get-tuple-element.50), channel_id=1, source_target_pairs={{1,0},{2,1},{3,2},{4,3},{5,4},{6,5},{7,6},{9,8},{10,9},{11,10},{12... | collective-permute-start | bytes 122888 | tf_op jit(solution)/shard_map/ppermute | solution.py:19
  363.3 1.7 copy-start.6
Sparse Core Ops, SparseCore 0:
  11.8 223.4 all-gather.1
  287.1 43.1 reduce-scatter.1
